TPU v7x, 32 devices: a whole 2x2x4 slice. The times are simulated.
32 devices in a mesh: row: 8 (over y, x, core), rep: 4 (over z).
Axes of the slice: x: 2, y: 2, z: 4, core: 2. Of those that a mesh axis runs over, the one named last changes fastest.
Arguments:
- features: bfloat16 [8192, 256], P('row'), may hold values from -6 to 6
- weight_self: bfloat16 [256, 256], replicated, may hold values from -0.375 to 0.375
- weight_neigh: bfloat16 [256, 256], replicated, may hold values from -0.375 to 0.375
- degrees: int32 [8192], P('row'), may hold values from 1 to 47
- tile_values: bfloat16 [8, 8, 48, 128, 128], P('row', 'rep'), may hold values from 0 to 1
- tile_blocks: int32 [8, 8, 48, 2], P('row', 'rep'), may hold values from 0 to 7
- tile_count: int32 [8, 8], P('row', 'rep'), may hold values from 1 to 48, as said below
- cotangent: bfloat16 [8192, 256], P(('row', 'rep')), may hold values from -6 to 6
Outputs:
- output: bfloat16 [8192, 256], P(('row', 'rep'))
- grad_self: float32 [256, 256], replicated
- grad_neigh: float32 [256, 256], replicated
- grad_features: bfloat16 [8192, 256], P(('row', 'rep'))
Inputs may be any that keep to these rules, and one draw needn't show every extreme that they name: `tile_count`: for some row index and section all 48 slots are live in every draw.
All inputs are finite; a program needn't handle non-finite values.
Results may differ from a plain program's by a relative error of at most 0.024.
Values may be sent and summed in bfloat16 or wider, within the bound.
A program may use at most 64 MiB of HBM per device.

v0:
```python
import jax
import jax.numpy as jnp
from jax import lax
from jax.sharding import PartitionSpec as P


def from_root(value, axis, source):
    kept = jnp.where(lax.axis_index(axis) == source, value, 0).astype(value.dtype)
    return lax.psum(kept, axis)


def hot_tables(blocks, count, nblk, slots):
    live = (jnp.arange(slots) < count).astype(jnp.float32)
    dest_hot = (blocks[:, 0][:, None] == jnp.arange(nblk)[None, :]).astype(jnp.float32) * live[
        :, None
    ]
    src_hot = (blocks[:, 1][:, None] == jnp.arange(nblk)[None, :]).astype(jnp.float32)
    return (dest_hot, src_hot)


def body(
    features, weight_self, weight_neigh, degrees, tile_values, tile_blocks, tile_count, cotangent
):
    rows, width = features.shape
    tile = tile_values.shape[3]
    slots = tile_values.shape[2]
    sections_here = tile_values.shape[1]
    nblk = rows // tile
    nrep = lax.axis_size("rep")
    share = rows // nrep
    rep_pos = lax.axis_index("rep")
    row_pos = lax.axis_index("row")
    partial_value = jnp.zeros((nblk, tile, width), jnp.float32)
    for section in range(sections_here):
        source = from_root(features, "row", rep_pos * sections_here + section)
        source_blocks = source.reshape(nblk, tile, width)
        dest_hot, src_hot = hot_tables(tile_blocks[0, section], tile_count[0, section], nblk, slots)
        picked = jnp.einsum(
            "tc,cif->tif",
            src_hot.astype(jnp.bfloat16),
            source_blocks,
            preferred_element_type=jnp.bfloat16,
        )
        prod = jnp.einsum(
            "tij,tjf->tif", tile_values[0, section], picked, preferred_element_type=jnp.float32
        )
        partial_value = partial_value + jnp.einsum("tb,tif->bif", dest_hot, prod)
    partial_value = partial_value.reshape(rows, width)
    degree_all = degrees.astype(jnp.float32)[:, None]
    degree_mine = lax.dynamic_slice_in_dim(degree_all, rep_pos * share, share, 0)
    feat_mine = lax.dynamic_slice_in_dim(features, rep_pos * share, share, 0)
    agg_part = lax.psum_scatter(partial_value, "rep", scatter_dimension=0, tiled=True)
    agg_mine = (agg_part / degree_mine).astype(jnp.bfloat16)
    pre = jnp.dot(feat_mine, weight_self, preferred_element_type=jnp.float32) + jnp.dot(
        agg_mine, weight_neigh, preferred_element_type=jnp.float32
    )
    sig = jax.nn.sigmoid(pre)
    gpre_mine = (cotangent.astype(jnp.float32) * sig * (1.0 + pre * (1.0 - sig))).astype(
        jnp.bfloat16
    )
    dagg_mine = (
        jnp.dot(gpre_mine, weight_neigh.T, preferred_element_type=jnp.float32) / degree_mine
    ).astype(jnp.bfloat16)
    dagg_all = lax.all_gather(dagg_mine, "rep", axis=0, tiled=True)
    output = jax.nn.silu(pre).astype(jnp.bfloat16)
    grad_self_part = jnp.dot(feat_mine.T, gpre_mine, preferred_element_type=jnp.float32)
    grad_neigh_part = jnp.dot(agg_mine.T, gpre_mine, preferred_element_type=jnp.float32)
    grad_self, grad_neigh = lax.psum((grad_self_part, grad_neigh_part), ("row", "rep"))
    dagg_blocks = dagg_all.reshape(nblk, tile, width)
    terms = []
    for section in range(sections_here):
        dest_hot, src_hot = hot_tables(tile_blocks[0, section], tile_count[0, section], nblk, slots)
        picked = jnp.einsum(
            "tb,bif->tif",
            dest_hot.astype(jnp.bfloat16),
            dagg_blocks,
            preferred_element_type=jnp.bfloat16,
        )
        contrib = jnp.einsum(
            "tij,tif->tjf", tile_values[0, section], picked, preferred_element_type=jnp.float32
        )
        terms.append(jnp.einsum("tc,tjf->cjf", src_hot, contrib).reshape(rows, width))
    stacked = jnp.stack(terms, 0)
    summed = lax.psum(stacked, "row")
    owned = lax.dynamic_index_in_dim(summed, row_pos % sections_here, 0, keepdims=False).astype(
        jnp.bfloat16
    )
    everyone = from_root(owned, "rep", row_pos // sections_here)
    back_mine = lax.dynamic_slice_in_dim(everyone, rep_pos * share, share, 0)
    grad_features = (
        jnp.dot(gpre_mine, weight_self.T, preferred_element_type=jnp.float32)
        + back_mine.astype(jnp.float32)
    ).astype(jnp.bfloat16)
    return (output, grad_self, grad_neigh, grad_features)


def solution(mesh):
    in_specs = (
        P("row", None),
        P(),
        P(),
        P("row"),
        P("row", "rep", None, None, None),
        P("row", "rep", None, None),
        P("row", "rep"),
        P(("row", "rep"), None),
    )
    out_specs = (P(("row", "rep"), None), P(), P(), P(("row", "rep"), None))
    return jax.shard_map(body, mesh=mesh, in_specs=in_specs, out_specs=out_specs, check_vma=False)
```

profile of v0, /device:TPU:0, one launch (start us, length us, event | category | flops | bytes accessed | tf_op | source)
XLA Modules:
  0.0 399.4 jit_solution(14081113110862203722)
XLA Ops:
  7.2 0.0 copy-start
  7.2 0.0 all-reduce.11.cloned.1.call-start
  7.2 0.0 copy-start.3
  7.2 2.3 broadcast_select_fusion.1
  9.5 0.0 all-reduce.11.cloned.1.call-update
  9.5 0.0 reduce-scatter.2.cloned.1.call-start
  9.6 1.3 fusion.78
  10.9 0.6 compare_convert_fusion
  11.6 0.0 copy-start.10
  11.6 0.7 compare_convert_fusion.1
  12.2 0.0 copy-start.12
  12.2 0.7 slice_bitcast_fusion.1
  13.0 57.8 %all-reduce.11.cloned.1.call-done = (bf16[8,128,256]{2,1,0:T(8,128)(2,1)}, bf16[8,128,256]{2,1,0:T(8,128)(2,1)}) async-done(((bf16[8,128,256]{2,1,0:T(8,128)(2,1)}, bf16[8,128,256]{2,1,0:T(8,128)(2,1)}), (bf16[8,128,256]{2,1,0:T(8,128)(2,1)}, bf16[8,128,256]{2,1,0:T(8,128)(2,1)})) %all-reduce.11.cloned.1.call-update) | async-done | bytes 1048592 | tf_op jit(solution)/shard_map/psum | solution.py:9
  70.7 2.1 fusion.31
  72.8 3.3 fusion.12
  76.0 3.8 copy.22
  79.9 0.0 copy-start.4
  79.9 2.2 fusion.33
  82.1 3.2 fusion.14
  85.3 4.9 %copy.19 = bf16[48,256,128]{1,0,2:T(8,128)(2,1)} copy(bf16[48,256,128]{2,1,0:T(8,128)(2,1)} %fusion.14) | data formatting | bytes 6291456 | tf_op jit(solution)/shard_map/tij,tjf->tif/dot_general | solution.py:44
  90.2 0.0 copy-done.10
  90.2 0.5 fusion.4
  90.8 1.4 copy-done.1
  92.1 0.5 fusion.24
  92.7 1.3 copy.14
  94.0 0.0 reduce-scatter.2.cloned.1.call-update
  94.0 0.0 all-reduce.7.cloned.1.call-start
  94.1 0.0 copy-done.9
  94.1 0.1 dynamic-slice.3
  94.2 1.1 fusion.41
  95.3 25.4 %reduce-scatter.2.cloned.1.call-done = f32[256,256]{1,0:T(8,128)} async-done(((f32[1024,256]{1,0:T(8,128)}), f32[256,256]{1,0:T(8,128)}) %reduce-scatter.2.cloned.1.call-update) | async-done | bytes 262160 | tf_op jit(solution)/shard_map/reduce_scatter | solution.py:52
  120.7 1.9 multiply_convert_fusion
  122.7 0.2 fusion.28
  122.9 16.2 %all_gather.3 = bf16[1024,256]{1,0:T(8,128)(2,1)S(1)} all-gather(bf16[256,256]{1,0:T(8,128)(2,1)S(1)} %fusion.28), channel_id=1, replica_groups=mesh['row'=8,'rep'=4] {'rep'}, dimensions={0}, use_global_device_ids=true | all-gather | bytes 655360 | tf_op jit(solution)/shard_map/all_gather | solution.py:64
  139.1 0.0 copy-done.13
  139.1 1.0 fusion.37
  140.1 0.0 copy-done.14
  140.1 2.7 fusion.35
  142.8 3.1 fusion.10
  145.9 3.8 copy.25
  149.8 0.0 copy-start.6
  149.8 0.5 fusion.2
  150.3 1.3 copy.15
  151.6 0.2 copy-done.2
  151.8 1.2 copy-done.6
  153.0 3.1 fusion.8
  156.1 3.8 copy.27
  159.9 0.5 fusion
  160.4 0.3 copy.16
  160.8 0.4 copy-done.7
  161.1 0.1 pad_maximum_fusion
  161.3 0.0 copy-start.15
  161.3 56.4 %all-reduce.12 = bf16[2,1024,256]{2,1,0:T(8,128)(2,1)S(1)} all-reduce(f32[2,1024,256]{2,1,0:T(8,128)S(1)} %pad_maximum_fusion), channel_id=1, replica_groups=mesh['row'=8,'rep'=4] {'row'}, use_global_device_ids=true, to_apply=%region_5.6 | all-reduce | flops 524288 | bytes 3145728 | tf_op jit(solution)/shard_map/psum | solution.py:84
  217.7 0.8 fusion.30
  218.5 0.0 all-reduce.7.cloned.1.call-update
  218.5 0.0 all-reduce.9.cloned.1.call-start
  218.6 1.8 fusion.39
  220.4 2.0 fusion.77
  222.4 0.0 all-reduce.9.cloned.1.call-update
  222.4 32.1 %all-reduce.7.cloned.1.call-done = bf16[1024,256]{1,0:T(8,128)(2,1)} async-done(((bf16[1024,256]{1,0:T(8,128)(2,1)}), bf16[1024,256]{1,0:T(8,128)(2,1)}) %all-reduce.7.cloned.1.call-update) | async-done | bytes 524304 | tf_op jit(solution)/shard_map/psum | solution.py:9
  254.5 1.8 fusion.27
  256.3 133.3 %all-reduce.9.cloned.1.call-done = (f32[256,256]{1,0:T(8,128)}, f32[256,256]{1,0:T(8,128)}) async-done(((f32[256,256]{1,0:T(8,128)}, f32[256,256]{1,0:T(8,128)}), (f32[256,256]{1,0:T(8,128)}, f32[256,256]{1,0:T(8,128)})) %all-reduce.9.cloned.1.call-update) | async-done | bytes 524304 | tf_op jit(solution)/shard_map/psum | solution.py:68
  389.6 1.7 copy.51
  391.2 1.7 copy.52
  (21 shorter events, 0.0 us)
Async XLA Ops:
  7.2 113.6 %copy-start = (bf16[256,256]{1,0:T(8,128)(2,1)S(1)}, bf16[256,256]{1,0:T(8,128)(2,1)}, u32[]{:S(2)}) copy-start(bf16[256,256]{1,0:T(8,128)(2,1)} %param.10) | copy-start | bytes 393220
  7.2 63.5 %all-reduce.11.cloned.1.call-start = ((), (), s32[]{:S(2)}) async-start(), calls=%async_computation.4 | async-start | bytes 2097152 | tf_op jit(solution)/shard_map/psum | solution.py:9
  7.2 65.5 %copy-start.3 = (bf16[1,2,48,128,128]{4,3,2,1,0:T(8,128)(2,1)S(1)}, bf16[1,2,48,128,128]{4,3,2,1,0:T(8,128)(2,1)}, u32[]{:S(2)}) copy-start(bf16[1,2,48,128,128]{4,3,2,1,0:T(8,128)(2,1)} %param.12) | copy-start | bytes 9437188
  9.5 111.2 %reduce-scatter.2.cloned.1.call-start = ((), (), s32[]{:S(2)}) async-start(), calls=%async_computation.1 | async-start | bytes 1310720 | tf_op jit(solution)/shard_map/reduce_scatter | solution.py:52
  11.6 78.7 %copy-start.10 = (bf16[48]{0:T(256)(128)(2,1)}, bf16[48]{0:T(256)(128)(2,1)S(1)}, u32[]{:S(2)}) copy-start(bf16[48]{0:T(256)(128)(2,1)S(1)} %compare_convert_fusion) | copy-start | bytes 292
  12.2 78.5 %copy-start.12 = (bf16[48]{0:T(256)(128)(2,1)}, bf16[48]{0:T(256)(128)(2,1)S(1)}, u32[]{:S(2)}) copy-start(bf16[48]{0:T(256)(128)(2,1)S(1)} %compare_convert_fusion.1) | copy-start | bytes 292
  79.9 2.2 copy-start.4
  90.2 1.9 copy-start.1
  92.1 1.9 copy-start.9
  92.1 2.1 copy-start.8
  92.7 28.1 %copy-start.16 = (bf16[256,256]{1,0:T(8,128)(2,1)S(1)}, bf16[256,256]{1,0:T(8,128)(2,1)}, u32[]{:S(2)}) copy-start(bf16[256,256]{1,0:T(8,128)(2,1)} %param.15) | copy-start | bytes 393220
  94.0 45.1 %copy-start.13 = (bf16[48]{0:T(256)(128)(2,1)S(1)}, bf16[48]{0:T(256)(128)(2,1)}, u32[]{:S(2)}) copy-start(bf16[48]{0:T(256)(128)(2,1)} %copy-done.12) | copy-start | bytes 292
  94.0 160.5 %all-reduce.7.cloned.1.call-start = ((), (), s32[]{:S(2)}) async-start(), calls=%async_computation.2 | async-start | bytes 1048576 | tf_op jit(solution)/shard_map/psum | solution.py:9
  94.2 45.9 %copy-start.14 = (f32[256]{0:T(256)}, f32[256]{0:T(256)S(1)}, u32[]{:S(2)}) copy-start(f32[256]{0:T(256)S(1)} %dynamic-slice.3) | copy-start | bytes 3076
  122.7 17.5 %copy-start.11 = (bf16[48]{0:T(256)(128)(2,1)S(1)}, bf16[48]{0:T(256)(128)(2,1)}, u32[]{:S(2)}) copy-start(bf16[48]{0:T(256)(128)(2,1)} %copy-done.10) | copy-start | bytes 292
  139.1 3.7 copy-start.5
  149.8 2.1 copy-start.2
  149.8 3.2 copy-start.6
  159.9 1.2 copy-start.7
  161.3 59.1 %copy-start.15 = (f32[256]{0:T(256)S(1)}, f32[256]{0:T(256)}, u32[]{:S(2)}) copy-start(f32[256]{0:T(256)} %copy-done.14) | copy-start | bytes 3076
  218.5 171.0 %all-reduce.9.cloned.1.call-start = ((), (), s32[]{:S(2)}) async-start(), calls=%async_computation.3 | async-start | bytes 1048576 | tf_op jit(solution)/shard_map/psum | solution.py:68
Sparse Core Ops, SparseCore 0:
  11.2 59.4 all-reduce.10
  94.1 26.5 reduce-scatter.1
  218.7 35.8 all-reduce.6
  260.4 129.1 all-reduce.8
where the time goes:
time: 400 us; the launch traced here: 399 us
  waiting for transfers between devices  249 us (62%)
  blocking collectives  72.6 us (18%)
  matrix products  31.5 us (8%)
  local copies, waits for them, and re-layouts  28 us (7%)
  between operations  14 us (4%)
  other arithmetic  4.54 us (1%)
    psum x1, waiting for transfers between devices, body(): lax.psum((grad_self_part, grad_neigh_part), ('row', 'rep'))  133 us
    psum x2, waiting for transfers between devices, from_root(): return lax.psum(kept, axis)  89.8 us
    psum x1, blocking collectives, body(): summed = lax.psum(stacked, 'row')  56.4 us
    reduce_scatter x1, waiting for transfers between devices, body(): lax.psum_scatter(partial_value, 'rep', scatter_dimension=0, tiled=True)  25.4 us
    all_gather x1, blocking collectives, body(): dagg_all = lax.all_gather(dagg_mine, 'rep', axis=0, tiled=True)  16.2 us
    dot_general x2, local copies, waits for them, and re-layouts, body(): jnp.einsum('tij,tjf->tif', tile_values[0, section], picked, preferred_ele...  8.77 us
  transfers between devices with their start and end apart: 4, of which 4 were waited for; matrix products, arithmetic and copies ran while one was open for 3% of the time, Pallas kernels for 0%

commit v1 on v0

--- a/solution.py
+++ b/solution.py
@@ -81,7 +81,9 @@
         )
         terms.append(jnp.einsum("tc,tjf->cjf", src_hot, contrib).reshape(rows, width))
     stacked = jnp.stack(terms, 0)
-    summed = lax.psum(stacked, "row")
+    summed = stacked
+    for hop in (1, 2, 4):
+        summed = summed + lax.ppermute(summed, "row", [(dev, dev ^ hop) for dev in range(8)])
     owned = lax.dynamic_index_in_dim(summed, row_pos % sections_here, 0, keepdims=False).astype(
         jnp.bfloat16
     )

time: 400 us -> 448 us (1.12)
  waiting for transfers between devices: 249 us -> 346 us
  blocking collectives: 72.6 us -> 16.2 us
    ppermute x0 -> x3, waiting for transfers between devices: none -> 95.8 us  [body(): lax.ppermute(summed, 'row', [(dev, dev ^ hop) for dev in range(8)])]
    psum x1 -> x0, blocking collectives: 56.4 us -> none  [body(): summed = lax.psum(stacked, 'row')]
  transfers between devices with their start and end apart: 4 -> 7, of which waited for: 4 -> 7; matrix products, arithmetic and copies ran while one was open for 3% -> 2% of each run, Pallas kernels for 0% -> 0%
where the time goes in v1:
time: 448 us; the launch traced here: 447 us
  waiting for transfers between devices  346 us (77%)
  matrix products  32.4 us (7%)
  local copies, waits for them, and re-layouts  28.5 us (6%)
  blocking collectives  16.2 us (4%)
  between operations  14 us (3%)
  other arithmetic  6.6 us (1%)
    psum x1, waiting for transfers between devices, body(): lax.psum((grad_self_part, grad_neigh_part), ('row', 'rep'))  133 us
    ppermute x3, waiting for transfers between devices, body(): lax.ppermute(summed, 'row', [(dev, dev ^ hop) for dev in range(8)])  95.8 us
    psum x2, waiting for transfers between devices, from_root(): return lax.psum(kept, axis)  91.9 us
    reduce_scatter x1, waiting for transfers between devices, body(): lax.psum_scatter(partial_value, 'rep', scatter_dimension=0, tiled=True)  25.5 us
    all_gather x1, blocking collectives, body(): dagg_all = lax.all_gather(dagg_mine, 'rep', axis=0, tiled=True)  16.2 us
  transfers between devices with their start and end apart: 7, of which 7 were waited for; matrix products, arithmetic and copies ran while one was open for 2% of the time, Pallas kernels for 0%

profile of v1, /device:TPU:0, one launch (start us, length us, event | category | flops | bytes accessed | tf_op | source)
XLA Modules:
  0.0 447.4 jit_solution(16339874532167293085)
XLA Ops:
  7.2 0.0 copy-start
  7.2 0.0 all-reduce.10.cloned.1.call-start
  7.2 0.0 copy-start.4
  7.3 2.3 broadcast_select_fusion.1
  9.6 0.0 all-reduce.10.cloned.1.call-update
  9.6 0.0 reduce-scatter.2.cloned.1.call-start
  9.6 1.3 fusion.80
  10.9 0.6 compare_convert_fusion
  11.6 0.0 copy-start.10
  11.6 0.7 compare_convert_fusion.1
  12.3 0.7 slice_bitcast_fusion.1
  13.0 57.7 %all-reduce.10.cloned.1.call-done = (bf16[8,128,256]{2,1,0:T(8,128)(2,1)}, bf16[8,128,256]{2,1,0:T(8,128)(2,1)}) async-done(((bf16[8,128,256]{2,1,0:T(8,128)(2,1)}, bf16[8,128,256]{2,1,0:T(8,128)(2,1)}), (bf16[8,128,256]{2,1,0:T(8,128)(2,1)}, bf16[8,128,256]{2,1,0:T(8,128)(2,1)})) %all-reduce.10.cloned.1.call-update) | async-done | bytes 1048592 | tf_op jit(solution)/shard_map/psum | solution.py:9
  70.7 2.1 fusion.32
  72.8 3.2 fusion.12
  76.0 3.8 copy.22
  79.9 0.0 copy-start.5
  79.9 2.2 fusion.34
  82.1 3.2 fusion.14
  85.3 5.0 %copy.19 = bf16[48,256,128]{1,0,2:T(8,128)(2,1)} copy(bf16[48,256,128]{2,1,0:T(8,128)(2,1)} %fusion.14) | data formatting | bytes 6291456 | tf_op jit(solution)/shard_map/tij,tjf->tif/dot_general | solution.py:44
  90.3 0.5 fusion.4
  90.8 1.4 copy-done.2
  92.2 0.5 fusion.24
  92.7 1.3 copy.14
  94.0 0.0 reduce-scatter.2.cloned.1.call-update
  94.0 0.0 all-reduce.6.cloned.1.call-start
  94.1 0.1 dynamic-slice.3
  94.2 1.1 fusion.42
  95.3 25.5 %reduce-scatter.2.cloned.1.call-done = f32[256,256]{1,0:T(8,128)} async-done(((f32[1024,256]{1,0:T(8,128)}), f32[256,256]{1,0:T(8,128)}) %reduce-scatter.2.cloned.1.call-update) | async-done | bytes 262160 | tf_op jit(solution)/shard_map/reduce_scatter | solution.py:52
  120.7 1.9 multiply_convert_fusion
  122.7 0.2 fusion.28
  122.9 16.2 %all_gather.3 = bf16[1024,256]{1,0:T(8,128)(2,1)S(1)} all-gather(bf16[256,256]{1,0:T(8,128)(2,1)S(1)} %fusion.28), channel_id=1, replica_groups=mesh['row'=8,'rep'=4] {'rep'}, dimensions={0}, use_global_device_ids=true | all-gather | bytes 655360 | tf_op jit(solution)/shard_map/all_gather | solution.py:64
  139.1 1.0 fusion.38
  140.1 2.6 fusion.36
  142.8 3.1 fusion.10
  145.9 3.8 copy.25
  149.8 0.0 copy-start.7
  149.8 0.5 fusion.2
  150.3 0.3 copy.15
  150.6 1.0 copy-done.3
  151.6 1.0 copy-done.7
  152.6 3.1 fusion.8
  155.7 5.0 %copy.27 = bf16[48,256,128]{1,0,2:T(8,128)(2,1)} copy(bf16[48,256,128]{2,1,0:T(8,128)(2,1)} %fusion.8) | data formatting | bytes 6291456 | tf_op jit(solution)/shard_map/tij,tif->tjf/dot_general | solution.py:79
  160.6 2.4 fusion
  163.0 0.3 copy.16
  163.4 0.1 pad_maximum_fusion
  163.5 0.1 collective-permute-start
  163.6 4.1 collective-permute-done
  167.8 0.3 fusion.79
  168.0 1.5 collective-permute-start.1
  169.5 46.2 %collective-permute-done.1 = f32[2,1024,256]{2,1,0:T(8,128)S(1)} collective-permute-done((f32[2,1024,256]{2,1,0:T(8,128)S(1)}, f32[2,1024,256]{2,1,0:T(8,128)S(1)}, u32[]{:S(2)}, u32[]{:S(2)}) %collective-permute-start.1) | collective-permute-done | bytes 2097184 | tf_op jit(solution)/shard_map/ppermute | solution.py:86
  215.8 0.4 fusion.89
  216.2 1.6 collective-permute-start.2
  217.8 45.4 %collective-permute-done.2 = f32[2,1024,256]{2,1,0:T(8,128)} collective-permute-done((f32[2,1024,256]{2,1,0:T(8,128)S(1)}, f32[2,1024,256]{2,1,0:T(8,128)}, u32[]{:S(2)}, u32[]{:S(2)}) %collective-permute-start.2) | collective-permute-done | bytes 2097184 | tf_op jit(solution)/shard_map/ppermute | solution.py:86
  263.2 2.2 fusion.31
  265.4 0.0 all-reduce.6.cloned.1.call-update
  265.4 0.0 all-reduce.8.cloned.1.call-start
  265.4 1.8 fusion.40
  267.3 1.0 fusion.78
  268.3 0.0 all-reduce.8.cloned.1.call-update
  268.3 34.2 %all-reduce.6.cloned.1.call-done = bf16[1024,256]{1,0:T(8,128)(2,1)} async-done(((bf16[1024,256]{1,0:T(8,128)(2,1)}), bf16[1024,256]{1,0:T(8,128)(2,1)}) %all-reduce.6.cloned.1.call-update) | async-done | bytes 524304 | tf_op jit(solution)/shard_map/psum | solution.py:9
  302.5 1.8 fusion.27
  304.3 133.3 %all-reduce.8.cloned.1.call-done = (f32[256,256]{1,0:T(8,128)}, f32[256,256]{1,0:T(8,128)}) async-done(((f32[256,256]{1,0:T(8,128)}, f32[256,256]{1,0:T(8,128)}), (f32[256,256]{1,0:T(8,128)}, f32[256,256]{1,0:T(8,128)})) %all-reduce.8.cloned.1.call-update) | async-done | bytes 524304 | tf_op jit(solution)/shard_map/psum | solution.py:68
  437.5 1.7 copy.49
  439.2 1.7 copy.50
  (30 shorter events, 0.1 us)
Async XLA Ops:
  7.2 113.6 %copy-start = (bf16[256,256]{1,0:T(8,128)(2,1)S(1)}, bf16[256,256]{1,0:T(8,128)(2,1)}, u32[]{:S(2)}) copy-start(bf16[256,256]{1,0:T(8,128)(2,1)} %param.10) | copy-start | bytes 393220
  7.2 63.5 %all-reduce.10.cloned.1.call-start = ((), (), s32[]{:S(2)}) async-start(), calls=%async_computation.4 | async-start | bytes 2097152 | tf_op jit(solution)/shard_map/psum | solution.py:9
  7.2 65.5 %copy-start.4 = (bf16[1,2,48,128,128]{4,3,2,1,0:T(8,128)(2,1)S(1)}, bf16[1,2,48,128,128]{4,3,2,1,0:T(8,128)(2,1)}, u32[]{:S(2)}) copy-start(bf16[1,2,48,128,128]{4,3,2,1,0:T(8,128)(2,1)} %param.12) | copy-start | bytes 9437188
  9.6 111.2 %reduce-scatter.2.cloned.1.call-start = ((), (), s32[]{:S(2)}) async-start(), calls=%async_computation.1 | async-start | bytes 1310720 | tf_op jit(solution)/shard_map/reduce_scatter | solution.py:52
  11.6 78.7 %copy-start.10 = (bf16[48]{0:T(256)(128)(2,1)}, bf16[48]{0:T(256)(128)(2,1)S(1)}, u32[]{:S(2)}) copy-start(bf16[48]{0:T(256)(128)(2,1)S(1)} %compare_convert_fusion) | copy-start | bytes 292
  12.3 78.5 %copy-start.12 = (bf16[48]{0:T(256)(128)(2,1)}, bf16[48]{0:T(256)(128)(2,1)S(1)}, u32[]{:S(2)}) copy-start(bf16[48]{0:T(256)(128)(2,1)S(1)} %compare_convert_fusion.1) | copy-start | bytes 292
  79.9 2.2 copy-start.5
  90.3 1.9 copy-start.2
  92.2 1.9 copy-start.9
  92.2 2.0 copy-start.8
  92.7 28.1 %copy-start.17 = (bf16[256,256]{1,0:T(8,128)(2,1)S(1)}, bf16[256,256]{1,0:T(8,128)(2,1)}, u32[]{:S(2)}) copy-start(bf16[256,256]{1,0:T(8,128)(2,1)} %param.15) | copy-start | bytes 393220
  94.0 45.1 %copy-start.13 = (bf16[48]{0:T(256)(128)(2,1)S(1)}, bf16[48]{0:T(256)(128)(2,1)}, u32[]{:S(2)}) copy-start(bf16[48]{0:T(256)(128)(2,1)} %copy-done.12) | copy-start | bytes 292
  94.0 208.5 %all-reduce.6.cloned.1.call-start = ((), (), s32[]{:S(2)}) async-start(), calls=%async_computation.2 | async-start | bytes 1048576 | tf_op jit(solution)/shard_map/psum | solution.py:9
  94.2 45.9 %copy-start.14 = (f32[256]{0:T(256)}, f32[256]{0:T(256)S(1)}, u32[]{:S(2)}) copy-start(f32[256]{0:T(256)S(1)} %dynamic-slice.3) | copy-start | bytes 3076
  122.7 17.4 %copy-start.11 = (bf16[48]{0:T(256)(128)(2,1)S(1)}, bf16[48]{0:T(256)(128)(2,1)}, u32[]{:S(2)}) copy-start(bf16[48]{0:T(256)(128)(2,1)} %copy-done.10) | copy-start | bytes 292
  139.1 3.7 copy-start.6
  149.7 1.9 copy-start.3
  149.8 2.8 copy-start.7
  163.5 4.2 collective-permute-start
  168.0 47.7 %collective-permute-start.1 = (f32[2,1024,256]{2,1,0:T(8,128)S(1)}, f32[2,1024,256]{2,1,0:T(8,128)S(1)}, u32[]{:S(2)}, u32[]{:S(2)}) collective-permute-start(f32[2,1024,256]{2,1,0:T(8,128)S(1)} %fusion.79), channel_id=1, source_target_pairs={{0,8},{4,12},{8,0},{12,4},{16,24},{20,28},{24,16},{28,20},{1,9},{5... | collective-permute-start | bytes 6291464 | tf_op jit(solution)/shard_map/ppermute | solution.py:86
  216.2 51.1 %copy-start.15 = (f32[256]{0:T(256)S(1)}, f32[256]{0:T(256)}, u32[]{:S(2)}) copy-start(f32[256]{0:T(256)} %copy-done.14) | copy-start | bytes 3076
  216.2 51.1 %copy-start.16 = (f32[256,256]{1,0:T(8,128)S(1)}, f32[256,256]{1,0:T(8,128)}, u32[]{:S(2)}) copy-start(f32[256,256]{1,0:T(8,128)} %reduce-scatter.2.cloned.1.call-done) | copy-start | bytes 786436
  216.2 47.0 %collective-permute-start.2 = (f32[2,1024,256]{2,1,0:T(8,128)S(1)}, f32[2,1024,256]{2,1,0:T(8,128)}, u32[]{:S(2)}, u32[]{:S(2)}) collective-permute-start(f32[2,1024,256]{2,1,0:T(8,128)S(1)} %fusion.89), channel_id=1, source_target_pairs={{0,16},{4,20},{8,24},{12,28},{16,0},{20,4},{24,8},{28,12},{1,17},{... | collective-permute-start | bytes 6291464 | tf_op jit(solution)/shard_map/ppermute | solution.py:86
  217.8 223.1 %copy-start.1 = (bf16[256,256]{1,0:T(8,128)(2,1)S(1)}, bf16[256,256]{1,0:T(8,128)(2,1)}, u32[]{:S(2)}) copy-start(bf16[256,256]{1,0:T(8,128)(2,1)} %param.10) | copy-start | bytes 393220
  265.4 172.1 %all-reduce.8.cloned.1.call-start = ((), (), s32[]{:S(2)}) async-start(), calls=%async_computation.3 | async-start | bytes 1048576 | tf_op jit(solution)/shard_map/psum | solution.py:68
Sparse Core Ops, SparseCore 0:
  11.2 59.4 all-reduce.9
  94.1 26.5 reduce-scatter.1
  265.5 36.9 all-reduce.5
  308.4 129.1 all-reduce.7
